TPU v7x, 32 devices: a whole 2x2x4 slice. The times are simulated.
32 devices in a mesh: rep: 8 (over z, x), batch: 4 (over y, core).
Axes of the slice: x: 2, y: 2, z: 4, core: 2. Of those that a mesh axis runs over, the one named last changes fastest.
Arguments:
- embed: bfloat16 [4096, 1024], P(('rep', 'batch')), may hold values from -9 to 9
- actions: int32 [4096, 5], P(('rep', 'batch')), may hold values from 0 to 17
- rewards: float32 [4096, 5], P(('rep', 'batch')), may hold values from -1 to 1
- ends: int32 [4096, 5], P(('rep', 'batch')), may hold values 0 or 1
- behaviour: float32 [4096, 5, 18], P(('rep', 'batch')), may hold values from -5 to 5
- w_hidden: bfloat16 [1024, 1024], replicated, may hold values from -0.1875 to 0.1875
- w_action: bfloat16 [18, 1024], replicated, may hold values from -3 to 3
- w_heads: bfloat16 [1024, 36], replicated, may hold values from -0.1875 to 0.1875
Outputs:
- grad_hidden: float32 [1024, 1024], replicated
- grad_action: float32 [18, 1024], replicated
- grad_heads: float32 [1024, 36], replicated
- targets: float32 [4096, 5], P(('rep', 'batch'))
All inputs are finite; a program needn't handle non-finite values. No bound on the sum of `ends` on one device may be relied on, other than what follows from the above.
Results may differ from a plain program's by a relative error of at most 0.0057.
Values sent between devices are 32-bit elements; how exact they have to be, the bound alone decides.
A program may use at most 64 MiB of HBM per device.

v0:
```python
import jax
import jax.numpy as jnp
from jax import lax
from jax.sharding import PartitionSpec as P

DISCOUNT = 0.997
TRACE_LAMBDA = 0.95
EPSILON = 1e-06


def unroll(emb_block, act_block, w_hidden, w_action, w_heads):
    act_count = w_action.shape[0]
    unroll_len = act_block.shape[1]
    onehot = (
        act_block[:, :, None] == jnp.arange(act_count, dtype=jnp.int32)[None, None, :]
    ).astype(jnp.bfloat16)
    hidden_state = emb_block.astype(jnp.float32)
    rounded = []
    squashed = []
    head_out = []
    for step in range(unroll_len):
        state_bf16 = hidden_state.astype(jnp.bfloat16)
        rounded.append(state_bf16)
        head_out.append(jnp.dot(state_bf16, w_heads, preferred_element_type=jnp.float32))
        preact = jnp.dot(state_bf16, w_hidden, preferred_element_type=jnp.float32)
        preact = preact + jnp.dot(onehot[:, step], w_action, preferred_element_type=jnp.float32)
        squash = jnp.tanh(preact)
        squashed.append(squash)
        hidden_state = hidden_state + squash
    state_bf16 = hidden_state.astype(jnp.bfloat16)
    head_out.append(jnp.dot(state_bf16, w_heads, preferred_element_type=jnp.float32))
    return (jnp.stack(head_out), rounded, squashed, onehot)


def estimates(head_out, actions, rewards, ends, behaviour):
    act_count = behaviour.shape[-1]
    unroll_len = actions.shape[1]
    logits = head_out[:, :, :act_count]
    qvalues = head_out[:, :, act_count:]
    exp_logits = jnp.exp(logits)
    policy = exp_logits / jnp.sum(exp_logits, axis=-1, keepdims=True)
    values = jnp.sum(policy * qvalues, axis=-1)
    onehot_f = (
        jnp.transpose(actions)[:, :, None] == jnp.arange(act_count, dtype=jnp.int32)[None, None, :]
    ).astype(jnp.float32)
    logpol = logits[:unroll_len] - jnp.log(jnp.sum(exp_logits[:unroll_len], axis=-1, keepdims=True))
    behave = jnp.transpose(behaviour, (1, 0, 2))
    behave_log = behave - jnp.log(jnp.sum(jnp.exp(behave), axis=-1, keepdims=True))
    ratios = jnp.exp(jnp.sum(onehot_f * (logpol - behave_log), axis=-1))
    clipped = jnp.minimum(1.0, ratios)
    not_ended = 1.0 - jnp.transpose(ends).astype(jnp.float32)
    td_error = jnp.transpose(rewards) + DISCOUNT * not_ended * values[1:] - values[:unroll_len]
    carried = jnp.zeros_like(values[0])
    collected = []
    for step in range(unroll_len - 1, -1, -1):
        carried = (
            clipped[step] * td_error[step]
            + DISCOUNT * TRACE_LAMBDA * not_ended[step] * clipped[step] * carried
        )
        collected.append(carried)
    collected = jnp.stack(collected[::-1])
    targets = values[:unroll_len] + collected
    advantage = qvalues[:unroll_len] - values[:unroll_len, :, None]
    return (policy[:unroll_len], onehot_f, targets, advantage)


def objective(head_out, onehot_f, targets, cmpo_policy, taken_weight, norm_scale):
    act_count = onehot_f.shape[-1]
    unroll_len = onehot_f.shape[0]
    logits = head_out[:unroll_len, :, :act_count]
    qvalues = head_out[:unroll_len, :, act_count:]
    logpol = logits - jnp.log(jnp.sum(jnp.exp(logits), axis=-1, keepdims=True))
    q_taken = jnp.sum(onehot_f * qvalues, axis=-1)
    value_term = 0.5 * (q_taken - targets) ** 2
    policy_term = -taken_weight * jnp.sum(onehot_f * logpol, axis=-1)
    regular = -jnp.sum(cmpo_policy * logpol, axis=-1)
    return jnp.sum(value_term + policy_term + regular) * norm_scale


def backward(cotangent, rounded, squashed, onehot, w_hidden, w_heads):
    unroll_len = len(squashed)
    hid = w_hidden.shape[0]
    grad_state = jnp.zeros(squashed[0].shape, jnp.float32)
    grad_hidden = jnp.zeros((hid, hid), jnp.float32)
    grad_action = jnp.zeros((hid, onehot.shape[-1]), jnp.float32)
    grad_heads = jnp.zeros(w_heads.shape, jnp.float32)
    for step in range(unroll_len - 1, -1, -1):
        grad_pre = (grad_state * (1.0 - squashed[step] * squashed[step])).astype(jnp.bfloat16)
        head_cot = cotangent[step].astype(jnp.bfloat16)
        grad_hidden = grad_hidden + jnp.dot(
            rounded[step].T, grad_pre, preferred_element_type=jnp.float32
        )
        grad_action = grad_action + jnp.dot(
            grad_pre.T, onehot[:, step], preferred_element_type=jnp.float32
        )
        grad_heads = grad_heads + jnp.dot(
            rounded[step].T, head_cot, preferred_element_type=jnp.float32
        )
        grad_state = grad_state + jnp.dot(grad_pre, w_hidden.T, preferred_element_type=jnp.float32)
        grad_state = grad_state + jnp.dot(head_cot, w_heads.T, preferred_element_type=jnp.float32)
    return (grad_hidden, grad_action, grad_heads)


def body(embed, actions, rewards, ends, behaviour, w_hidden, w_action, w_heads):
    rows_here = embed.shape[0]
    unroll_len = actions.shape[1]
    act_count = w_action.shape[0]
    groups = lax.axis_size("batch")
    devices = lax.axis_size("rep") * groups
    head_out, rounded, squashed, onehot = unroll(embed, actions, w_hidden, w_action, w_heads)
    policy, onehot_f, targets, advantage = estimates(head_out, actions, rewards, ends, behaviour)
    spread = lax.psum(jnp.sum(advantage * advantage), "batch")
    spread_scale = jnp.sqrt(spread / (groups * rows_here * unroll_len * act_count) + EPSILON)
    weights = jnp.exp(jnp.clip(advantage / spread_scale, -1.0, 1.0))
    norm_mass = jnp.sum(policy * weights, axis=-1)
    mass_sum = lax.psum(jnp.sum(norm_mass), "batch")
    mean_mass = mass_sum / (groups * rows_here * unroll_len)
    cmpo_policy = policy * weights / norm_mass[:, :, None]
    taken_weight = jnp.sum(onehot_f * weights, axis=-1) / mean_mass
    cotangent = jax.grad(objective)(
        head_out,
        onehot_f,
        targets,
        cmpo_policy,
        taken_weight,
        1.0 / (devices * rows_here * unroll_len),
    )
    grad_hidden, grad_action, grad_heads = backward(
        cotangent, rounded, squashed, onehot, w_hidden, w_heads
    )
    grad_hidden, grad_action, grad_heads = lax.psum(
        (grad_hidden, grad_action, grad_heads), ("rep", "batch")
    )
    return (grad_hidden, grad_action.T, grad_heads, targets.T)


def solution(mesh):
    placed = (
        P(("rep", "batch"), None),
        P(("rep", "batch"), None),
        P(("rep", "batch"), None),
        P(("rep", "batch"), None),
        P(("rep", "batch"), None, None),
        P(),
        P(),
        P(),
    )
    return jax.shard_map(
        body,
        mesh=mesh,
        in_specs=placed,
        out_specs=(P(), P(), P(), P(("rep", "batch"), None)),
        check_vma=False,
    )
```

profile of v0, /device:TPU:0, one launch (start us, length us, event | category | flops | bytes accessed | tf_op | source)
XLA Modules:
  0.0 216.6 jit_solution(16951233208367975323)
XLA Ops:
  7.2 0.9 iota_compare_fusion.1
  8.1 0.7 copy-done
  8.8 1.4 fusion.52
  11.7 1.1 fusion.48
  13.6 0.4 fusion.56
  14.3 0.8 fusion.41
  15.1 1.6 fusion.45
  16.7 2.7 %fusion.46 = f32[1024,1024]{1,0:T(8,128)} fusion(bf16[128,1024]{1,0:T(8,128)(2,1)S(1)} %get-tuple-element.46, f32[128,1024]{1,0:T(8,128)S(1)} %fusion.4), kind=kOutput, calls=%fused_computation.125 | convolution fusion | flops 268959744 | bytes 4980736 | tf_op jit(solution)/shard_map/dot_general | solution.py:90
  21.0 0.7 slice_exponential_fusion
  21.6 0.6 multiply_reduce_fusion
  22.3 9.0 %psum.35 = f32[]{:T(128)} all-reduce(f32[]{:T(128)} %multiply_reduce_fusion), channel_id=1, replica_groups=mesh['rep'=8,'batch'=4] {'batch'}, use_global_device_ids=true, to_apply=%region_7.8 | all-reduce | flops 1 | bytes 8 | tf_op jit(solution)/shard_map/psum | solution.py:112
  32.1 2.2 %select_reduce_fusion.1 = (f32[5,128]{1,0:T(8,128)S(1)}, f32[5,128]{1,0:T(8,128)}, f32[5,128]{1,0:T(8,128)}, f32[]{:T(128)}, f32[5,128,18]{1,2,0:T(8,128)}) fusion(f32[5,128,36]{1,2,0:T(8,128)} %copy-done.14, s32[5,128]{1,0:T(8,128)S(1)} %bitcast.143, f32[]{:T(128)S(6)} %sqrt.3, f32[5,128]{1,0:T(8,128)S(1)} %get-tuple-element.40, ...), kind=kLoop, calls=%fused_computation.71 | loop fusion | flops 124799 | bytes 197128 | tf_op jit(solution)/shard_map/jvp()/reduce_sum | solution.py:73
  34.2 6.4 %psum.36 = f32[]{:T(128)} all-reduce(f32[]{:T(128)} %get-tuple-element.25), channel_id=1, replica_groups=mesh['rep'=8,'batch'=4] {'batch'}, use_global_device_ids=true, to_apply=%region_11.12 | all-reduce | flops 1 | bytes 8 | tf_op jit(solution)/shard_map/psum | solution.py:116
  40.7 0.6 add_bitcast_fusion
  42.1 0.8 negate_multiply_fusion
  42.8 0.9 fusion.50
  43.8 0.7 negate_divide_fusion
  44.5 0.9 multiply_add_fusion
  45.3 1.1 fusion.60
  47.0 0.8 fusion.10
  48.1 0.7 fusion.57
  48.9 0.8 convolution_add_fusion.6
  50.2 0.7 fusion.58
  50.9 0.8 convolution_add_fusion.5
  52.2 0.7 fusion.59
  53.0 0.8 convolution_add_fusion.4
  54.6 0.8 fusion.11
  55.4 3.1 %bitcast_add_fusion = f32[1024,1024]{1,0:T(8,128)} fusion(f32[1024,1024]{1,0:T(8,128)S(1)} %fusion.59, f32[1024,1024]{1,0:T(8,128)S(1)} %fusion.58, f32[1024,1024]{1,0:T(8,128)S(1)} %copy-done.1, f32[1024,1024]{1,0:T(8,128)S(1)} %fusion.57, bf16[128,1024]{1,0:T(8,128)(2,1)S(1)} %fusion.9, bf16[128,1024]{1,0:T(8,128)(2,1)S(1)} %copy-done.2), kind=kOutput, calls=%fused_computation.3 | convolution fusion | flops 272629760 | bytes 21495808 | tf_op jit(solution)/shard_map/dot_general | solution.py:90
  58.4 145.2 %all-reduce.5.cloned.1.call-done = (f32[1024,1024]{1,0:T(8,128)}, f32[18,1024]{1,0:T(8,128)}, f32[1024,36]{0,1:T(8,128)}) async-done(((f32[1024,1024]{1,0:T(8,128)}, f32[18,1024]{1,0:T(8,128)}, f32[1024,36]{0,1:T(8,128)}), (f32[1024,1024]{1,0:T(8,128)}, f32[18,1024]{1,0:T(8,128)}, f32[1024,36]{0,1:T(8,128)})) %all-reduce.5.cloned.1.call-update) | async-done | bytes 4415504 | tf_op jit(solution)/shard_map/psum | solution.py:131
  203.6 4.8 %copy.28 = f32[1024,1024]{1,0:T(8,128)} copy(f32[1024,1024]{1,0:T(8,128)} %get-tuple-element.57) | data formatting | bytes 8388608
  208.4 0.6 copy.29
  209.1 0.7 copy.30
  (81 shorter events, 6.5 us)
Async XLA Ops:
  7.2 1.6 copy-start
  7.2 3.0 %copy-start.2 = (bf16[128,1024]{1,0:T(8,128)(2,1)S(1)}, bf16[128,1024]{1,0:T(8,128)(2,1)}, u32[]{:S(2)}) copy-start(bf16[128,1024]{1,0:T(8,128)(2,1)} %param.8) | copy-start | bytes 786436
  7.2 3.0 %copy-start.13 = (bf16[18,1024]{1,0:T(8,128)(2,1)S(1)}, bf16[18,1024]{1,0:T(8,128)(2,1)}, u32[]{:S(2)}) copy-start(bf16[18,1024]{1,0:T(8,128)(2,1)} %param.14) | copy-start | bytes 110596
  7.2 196.4 %all-reduce.5.cloned.1.call-start = ((), (), s32[]{:S(2)}) async-start(), calls=%async_computation | async-start | bytes 8912896 | tf_op jit(solution)/shard_map/psum | solution.py:131
  8.8 5.5 %copy-start.17 = (pred[128,5,18]{0,2,1:T(8,128)(4,1)}, pred[128,5,18]{0,2,1:T(8,128)(4,1)S(1)}, u32[]{:S(2)}) copy-start(pred[128,5,18]{0,2,1:T(8,128)(4,1)S(1)} %iota_compare_fusion.1) | copy-start | bytes 34564
  10.5 9.4 %copy-start.4 = (bf16[128,1024]{1,0:T(8,128)(2,1)}, bf16[128,1024]{1,0:T(8,128)(2,1)S(1)}, u32[]{:S(2)}) copy-start(bf16[128,1024]{1,0:T(8,128)(2,1)S(1)} %get-tuple-element.41) | copy-start | bytes 786436
  11.2 1.5 copy-start.7
  13.5 7.0 %copy-start.6 = (bf16[128,1024]{1,0:T(8,128)(2,1)}, bf16[128,1024]{1,0:T(8,128)(2,1)S(1)}, u32[]{:S(2)}) copy-start(bf16[128,1024]{1,0:T(8,128)(2,1)S(1)} %get-tuple-element.46) | copy-start | bytes 786436
  13.5 7.2 %copy-start.9 = (f32[128,1024]{1,0:T(8,128)}, f32[128,1024]{1,0:T(8,128)S(1)}, u32[]{:S(2)}) copy-start(f32[128,1024]{1,0:T(8,128)S(1)} %get-tuple-element.47) | copy-start | bytes 1572868
  16.7 2.8 %copy-start.22 = (s32[128,5]{0,1:T(8,128)S(1)}, s32[128,5]{0,1:T(8,128)}, u32[]{:S(2)}) copy-start(s32[128,5]{0,1:T(8,128)} %param.11) | copy-start | bytes 7684
  16.7 2.8 %copy-start.21 = (f32[128,5,18]{0,2,1:T(8,128)S(1)}, f32[128,5,18]{0,2,1:T(8,128)}, u32[]{:S(2)}) copy-start(f32[128,5,18]{0,2,1:T(8,128)} %param.12) | copy-start | bytes 138244
  16.7 2.9 %copy-start.3 = (bf16[1024,36]{0,1:T(8,128)(2,1)S(1)}, bf16[1024,36]{0,1:T(8,128)(2,1)}, u32[]{:S(2)}) copy-start(bf16[1024,36]{0,1:T(8,128)(2,1)} %param.15) | copy-start | bytes 221188
  19.5 2.1 copy-start.23
  19.5 2.8 %copy-start.20 = (s32[128,5]{0,1:T(8,128)S(1)}, s32[128,5]{0,1:T(8,128)}, u32[]{:S(2)}) copy-start(s32[128,5]{0,1:T(8,128)} %param.9) | copy-start | bytes 7684
  20.7 1.6 copy-start.14
  42.0 4.8 %copy-start.5 = (bf16[128,1024]{1,0:T(8,128)(2,1)S(1)}, bf16[128,1024]{1,0:T(8,128)(2,1)}, u32[]{:S(2)}) copy-start(bf16[128,1024]{1,0:T(8,128)(2,1)} %copy-done.4) | copy-start | bytes 786436
  42.0 5.8 %copy-start.10 = (f32[128,1024]{1,0:T(8,128)S(1)}, f32[128,1024]{1,0:T(8,128)}, u32[]{:S(2)}) copy-start(f32[128,1024]{1,0:T(8,128)} %copy-done.9) | copy-start | bytes 1572868
  42.0 5.8 %copy-start.12 = (f32[128,1024]{1,0:T(8,128)S(1)}, f32[128,1024]{1,0:T(8,128)}, u32[]{:S(2)}) copy-start(f32[128,1024]{1,0:T(8,128)} %fusion.45) | copy-start | bytes 1572868
  48.8 1.0 copy-start.11
  50.9 1.0 copy-start.8
  52.9 1.1 copy-start.15
  52.9 1.1 copy-start.18
  52.9 2.4 %copy-start.1 = (f32[1024,1024]{1,0:T(8,128)S(1)}, f32[1024,1024]{1,0:T(8,128)}, u32[]{:S(2)}) copy-start(f32[1024,1024]{1,0:T(8,128)} %fusion.46) | copy-start | bytes 12582916
  203.6 4.8 %copy-start.19 = (f32[18,1024]{1,0:T(8,128)S(1)}, f32[18,1024]{1,0:T(8,128)}, u32[]{:S(2)}) copy-start(f32[18,1024]{1,0:T(8,128)} %get-tuple-element.58) | copy-start | bytes 221188
  203.6 5.5 %copy-start.16 = (f32[1024,36]{0,1:T(8,128)S(1)}, f32[1024,36]{0,1:T(8,128)}, u32[]{:S(2)}) copy-start(f32[1024,36]{0,1:T(8,128)} %get-tuple-element.59) | copy-start | bytes 442372
Sparse Core Ops, SparseCore 0:
  58.6 145.0 all-reduce.4
where the time goes:
time: 217 us
  waiting for transfers between devices  145 us (67%)
  matrix products  24.2 us (11%)
  between operations  15.9 us (7%)
  blocking collectives  15.5 us (7%)
  other arithmetic  8.42 us (4%)
  local copies, waits for them, and re-layouts  7.38 us (3%)
    psum x1, waiting for transfers between devices, body(): lax.psum((grad_hidden, grad_action, grad_heads), ('rep', 'batch'))  145 us
    psum x1, blocking collectives, body(): spread = lax.psum(jnp.sum(advantage * advantage), 'batch')  9.04 us
    dot_general x5, matrix products, backward(): jnp.dot(rounded[step].T, grad_pre, preferred_element_type=jnp.float32)  7.97 us
    unnamed x51, local copies, waits for them, and re-layouts  7.36 us
    psum x1, blocking collectives, body(): mass_sum = lax.psum(jnp.sum(norm_mass), 'batch')  6.44 us
  transfers between devices with their start and end apart: 1, of which 1 were waited for; matrix products, arithmetic and copies ran while one was open for 0% of the time, Pallas kernels for 0%

commit v1 on v0

--- a/solution.py
+++ b/solution.py
@@ -129,7 +129,7 @@
         cotangent, rounded, squashed, onehot, w_hidden, w_heads
     )
     grad_hidden, grad_action, grad_heads = lax.psum(
-        (grad_hidden, grad_action, grad_heads), ("rep", "batch")
+        lax.psum((grad_hidden, grad_action, grad_heads), "batch"), "rep"
     )
     return (grad_hidden, grad_action.T, grad_heads, targets.T)
 

time: 217 us -> 329 us (1.52)
  waiting for transfers between devices: 145 us -> 257 us
    psum x1 -> x2, waiting for transfers between devices: 145 us -> 257 us  [the longest x1 167 us: body(): lax.psum(lax.psum((grad_hidden, grad_action, grad_heads), 'batch'), 'rep')]
  transfers between devices with their start and end apart: 1 -> 2, of which waited for: 1 -> 2; matrix products, arithmetic and copies ran while one was open for 0% -> 0% of each run, Pallas kernels for 0% -> 0%
where the time goes in v1:
time: 329 us
  waiting for transfers between devices  257 us (78%)
  matrix products  24.2 us (7%)
  between operations  15.8 us (5%)
  blocking collectives  15.5 us (5%)
  other arithmetic  8.41 us (3%)
  local copies, waits for them, and re-layouts  7.38 us (2%)
    psum x1, waiting for transfers between devices, body(): lax.psum(lax.psum((grad_hidden, grad_action, grad_heads), 'batch'), 'rep')  167 us
    psum x1, waiting for transfers between devices, body(): lax.psum((grad_hidden, grad_action, grad_heads), 'batch')  90.3 us
    psum x1, blocking collectives, body(): spread = lax.psum(jnp.sum(advantage * advantage), 'batch')  9.04 us
    dot_general x5, matrix products, backward(): jnp.dot(rounded[step].T, grad_pre, preferred_element_type=jnp.float32)  7.97 us
    unnamed x51, local copies, waits for them, and re-layouts  7.36 us
  transfers between devices with their start and end apart: 2, of which 2 were waited for; matrix products, arithmetic and copies ran while one was open for 0% of the time, Pallas kernels for 0%

profile of v1, /device:TPU:0, one launch (start us, length us, event | category | flops | bytes accessed | tf_op | source)
XLA Modules:
  0.0 328.7 jit_solution(7001495794788595772)
XLA Ops:
  7.2 0.9 iota_compare_fusion.1
  8.1 0.7 copy-done
  8.8 1.4 fusion.51
  11.7 1.1 fusion.47
  14.3 0.8 fusion.40
  15.1 1.6 fusion.44
  16.8 2.7 fusion.45
  21.0 0.7 slice_exponential_fusion
  21.6 0.6 multiply_reduce_fusion
  22.3 9.0 %psum.56 = f32[]{:T(128)} all-reduce(f32[]{:T(128)} %multiply_reduce_fusion), channel_id=1, replica_groups=mesh['rep'=8,'batch'=4] {'batch'}, use_global_device_ids=true, to_apply=%region_7.8 | all-reduce | flops 1 | bytes 8 | tf_op jit(solution)/shard_map/psum | solution.py:112
  32.1 2.2 select_reduce_fusion.1
  34.2 6.4 %psum.57 = f32[]{:T(128)} all-reduce(f32[]{:T(128)} %get-tuple-element.28), channel_id=1, replica_groups=mesh['rep'=8,'batch'=4] {'batch'}, use_global_device_ids=true, to_apply=%region_11.12 | all-reduce | flops 1 | bytes 8 | tf_op jit(solution)/shard_map/psum | solution.py:116
  40.7 0.6 add_bitcast_fusion
  42.0 0.8 negate_multiply_fusion
  42.8 0.9 fusion.49
  43.7 0.7 negate_divide_fusion
  44.4 0.9 multiply_add_fusion
  45.3 1.1 fusion.59
  46.9 0.8 fusion.10
  48.0 0.7 fusion.56
  48.8 0.8 convolution_add_fusion.6
  50.1 0.7 fusion.57
  50.8 0.8 convolution_add_fusion.5
  52.1 0.7 fusion.58
  52.9 0.8 convolution_add_fusion.4
  54.5 0.8 convolution_add_fusion.15
  55.3 3.1 bitcast_add_fusion
  58.4 90.3 %all-reduce.9.cloned.1.call-done = (f32[1024,1024]{1,0:T(8,128)}, f32[1024,18]{0,1:T(8,128)}, f32[1024,36]{0,1:T(8,128)}) async-done(((f32[1024,1024]{1,0:T(8,128)}, f32[1024,18]{0,1:T(8,128)}, f32[1024,36]{0,1:T(8,128)}), (f32[1024,1024]{1,0:T(8,128)}, f32[1024,18]{0,1:T(8,128)}, f32[1024,36]{0,1:T(8,128)})) %all-reduce.9.cloned.1.call-update) | async-done | bytes 4415504 | tf_op jit(solution)/shard_map/psum | solution.py:132
  148.7 167.1 %all-reduce.7.cloned.1.call-done = (f32[1024,1024]{1,0:T(8,128)}, f32[18,1024]{1,0:T(8,128)}, f32[1024,36]{0,1:T(8,128)}) async-done(((f32[1024,1024]{1,0:T(8,128)}, f32[18,1024]{1,0:T(8,128)}, f32[1024,36]{0,1:T(8,128)}), (f32[1024,1024]{1,0:T(8,128)}, f32[18,1024]{1,0:T(8,128)}, f32[1024,36]{0,1:T(8,128)})) %all-reduce.7.cloned.1.call-update) | async-done | bytes 4415504 | tf_op jit(solution)/shard_map/psum | solution.py:131
  315.8 4.8 %copy.31 = f32[1024,1024]{1,0:T(8,128)} copy(f32[1024,1024]{1,0:T(8,128)} %get-tuple-element.60) | data formatting | bytes 8388608
  320.6 0.6 copy.32
  321.2 0.7 copy.33
  (84 shorter events, 7.0 us)
Async XLA Ops:
  7.2 1.6 copy-start
  7.2 3.0 copy-start.2
  7.2 3.0 copy-start.13
  7.2 141.5 %all-reduce.9.cloned.1.call-start = ((), (), s32[]{:S(2)}) async-start(), calls=%async_computation.1 | async-start | bytes 8912896 | tf_op jit(solution)/shard_map/psum | solution.py:132
  8.8 5.5 %copy-start.17 = (pred[128,5,18]{0,2,1:T(8,128)(4,1)}, pred[128,5,18]{0,2,1:T(8,128)(4,1)S(1)}, u32[]{:S(2)}) copy-start(pred[128,5,18]{0,2,1:T(8,128)(4,1)S(1)} %iota_compare_fusion.1) | copy-start | bytes 34564
  10.5 9.4 %copy-start.4 = (bf16[128,1024]{1,0:T(8,128)(2,1)}, bf16[128,1024]{1,0:T(8,128)(2,1)S(1)}, u32[]{:S(2)}) copy-start(bf16[128,1024]{1,0:T(8,128)(2,1)S(1)} %get-tuple-element.44) | copy-start | bytes 786436
  11.2 1.6 copy-start.7
  13.5 7.0 %copy-start.6 = (bf16[128,1024]{1,0:T(8,128)(2,1)}, bf16[128,1024]{1,0:T(8,128)(2,1)S(1)}, u32[]{:S(2)}) copy-start(bf16[128,1024]{1,0:T(8,128)(2,1)S(1)} %get-tuple-element.49) | copy-start | bytes 786436
  13.6 7.2 %copy-start.9 = (f32[128,1024]{1,0:T(8,128)}, f32[128,1024]{1,0:T(8,128)S(1)}, u32[]{:S(2)}) copy-start(f32[128,1024]{1,0:T(8,128)S(1)} %get-tuple-element.50) | copy-start | bytes 1572868
  16.7 2.8 copy-start.22
  16.7 2.8 copy-start.21
  16.7 2.9 copy-start.3
  19.5 2.1 copy-start.23
  19.5 2.8 copy-start.20
  20.7 1.6 copy-start.14
  42.0 4.8 %copy-start.5 = (bf16[128,1024]{1,0:T(8,128)(2,1)S(1)}, bf16[128,1024]{1,0:T(8,128)(2,1)}, u32[]{:S(2)}) copy-start(bf16[128,1024]{1,0:T(8,128)(2,1)} %copy-done.4) | copy-start | bytes 786436
  42.0 5.8 %copy-start.10 = (f32[128,1024]{1,0:T(8,128)S(1)}, f32[128,1024]{1,0:T(8,128)}, u32[]{:S(2)}) copy-start(f32[128,1024]{1,0:T(8,128)} %copy-done.9) | copy-start | bytes 1572868
  42.0 5.8 %copy-start.12 = (f32[128,1024]{1,0:T(8,128)S(1)}, f32[128,1024]{1,0:T(8,128)}, u32[]{:S(2)}) copy-start(f32[128,1024]{1,0:T(8,128)} %fusion.44) | copy-start | bytes 1572868
  48.8 1.0 copy-start.11
  50.8 1.0 copy-start.8
  52.8 1.1 copy-start.15
  52.9 1.1 copy-start.18
  52.9 2.4 copy-start.1
  58.4 257.4 %all-reduce.7.cloned.1.call-start = ((), (), s32[]{:S(2)}) async-start(), calls=%async_computation | async-start | bytes 8912896 | tf_op jit(solution)/shard_map/psum | solution.py:131
  315.8 4.8 %copy-start.19 = (f32[18,1024]{1,0:T(8,128)S(1)}, f32[18,1024]{1,0:T(8,128)}, u32[]{:S(2)}) copy-start(f32[18,1024]{1,0:T(8,128)} %get-tuple-element.61) | copy-start | bytes 221188
  315.8 5.5 %copy-start.16 = (f32[1024,36]{0,1:T(8,128)S(1)}, f32[1024,36]{0,1:T(8,128)}, u32[]{:S(2)}) copy-start(f32[1024,36]{0,1:T(8,128)} %get-tuple-element.62) | copy-start | bytes 442372
Sparse Core Ops, SparseCore 0:
  58.5 90.1 all-reduce.8
  152.6 163.1 all-reduce.6
